TPU v7x, 128 devices: a whole 4x4x4 slice. The times are simulated.
128 devices in a mesh: tiles: 64 (over y, z_hi, x, core), vec: 2 (over z_lo).
Axes of the slice: x: 4, y: 4, z: 4 (z_hi: 2, z_lo: 2; z = z_hi * 2 + z_lo), core: 2. Of those that a mesh axis runs over, the one named last changes fastest.
Arguments:
- omega: float32 [128, 4, 512, 128], P('vec', None, 'tiles'), may hold values from -24 to 24
- conductance: float32 [3, 4, 512, 128], P(None, None, 'tiles'), may hold values from 0.02 to 0.16
- wet: int32 [512, 128], P('tiles'), may hold values 0 or 1
- volume: float32 [512, 128], P('tiles'), may hold values from 0.3 to 27, as said below
- face_runs: int32 [64, 4], P('tiles'), may hold values from 0 to 128, as said below
Outputs:
- diffused: float32 [128, 4, 512, 128], P('vec', None, 'tiles')
- r_factor: float32 [128, 128], replicated
Inputs may be any that keep to these rules, and one draw needn't show every extreme that they name: `face_runs`: tiles in tile row 0 have a closed lower row face and tiles in tile column 0 a closed lower column face (length 0); every other run lies within its face, covers at least half of it, and some tiles have fully open faces. Positive cell volume weights.
All inputs are finite; a program needn't handle non-finite values. No bound on the sum of `wet` on one device may be relied on, other than what follows from the above.
Results may differ from a plain program's by a relative error of at most 0.00005.
Values sent between devices are 32-bit elements; how exact they have to be, the bound alone decides.
A program may use at most 64 MiB of HBM per device.

v0:
```python
import jax
import jax.numpy as jnp
from jax import lax
from jax.sharding import PartitionSpec as P

TGY = 8
ITERS = 4


def shifted(value, axis, steps):
    count = lax.axis_size(axis)
    first, last = (max(0, -steps), min(count, count - steps))
    return lax.ppermute(value, axis, [(source, source + steps) for source in range(first, last)])


def diffuse(field, statics):
    cond_x = statics[0]
    cond_y = statics[1]
    cond_z = statics[2]
    wet_cells = statics[3]
    flux_x = cond_x[:, 1:, :] * (field[:, :, 1:, :] - field[:, :, :-1, :])
    flux_y = cond_y[:, :, 1:] * (field[:, :, :, 1:] - field[:, :, :, :-1])
    flux_z = cond_z[1:] * (field[:, 1:] - field[:, :-1])
    zero_level = jnp.zeros_like(field[:, :1])
    flux_z = jnp.concatenate([zero_level, flux_z, zero_level], axis=1)
    change = flux_x[:, :, 1:, 1:-1] - flux_x[:, :, :-1, 1:-1]
    change = change + flux_y[:, :, 1:-1, 1:] - flux_y[:, :, 1:-1, :-1]
    change = change + (flux_z[:, 1:] - flux_z[:, :-1])[:, :, 1:-1, 1:-1]
    return wet_cells[:, 1:-1, 1:-1] * (field[:, :, 1:-1, 1:-1] + change)


def moving(values, offset):
    return shifted(values, "tiles", offset)


def fixed_rim(values, offset):
    return shifted(values, "tiles", offset)


def extend(values, margin, neighbour):
    lower_rim = neighbour(values[:, :, -margin:, :], TGY)
    upper_rim = neighbour(values[:, :, :margin, :], -TGY)
    stacked = jnp.concatenate([lower_rim, values, upper_rim], axis=2)
    left_rim = neighbour(stacked[:, :, :, -margin:], 1)
    right_rim = neighbour(stacked[:, :, :, :margin], -1)
    return jnp.concatenate([left_rim, stacked, right_rim], axis=3)


def shards(omega, conductance, wet, volume, face_runs):
    levels = omega.shape[1]
    tile_rows = omega.shape[2]
    tile_cols = omega.shape[3]
    row_ids = lax.broadcasted_iota(jnp.int32, (tile_rows, tile_cols), 0)
    col_ids = lax.broadcasted_iota(jnp.int32, (tile_rows, tile_cols), 1)
    runs = face_runs[0]
    open_x = (col_ids >= runs[0]) & (col_ids < runs[0] + runs[1])
    factor_x = jnp.where(row_ids == 0, open_x.astype(jnp.float32), jnp.float32(1.0))
    open_y = (row_ids >= runs[2]) & (row_ids < runs[2] + runs[3])
    factor_y = jnp.where(col_ids == 0, open_y.astype(jnp.float32), jnp.float32(1.0))
    level_ids = lax.broadcasted_iota(jnp.int32, (levels, 1, 1), 0)
    cond_z = conductance[2] * (level_ids > 0).astype(jnp.float32)
    wet_float = wet.astype(jnp.float32)
    statics = jnp.stack(
        [
            conductance[0] * factor_x[None],
            conductance[1] * factor_y[None],
            cond_z,
            jnp.broadcast_to(wet_float[None], (levels, tile_rows, tile_cols)),
        ]
    )
    margin = 1
    statics_wide = extend(statics, margin, fixed_rim)
    field = wet_float[None, None] * omega
    for block_index in range(ITERS // margin):
        grown = extend(field, margin, moving)
        current = statics_wide
        grown = diffuse(grown, current)
        current = current[:, :, 1:-1, 1:-1]
        field = grown
    regrouped = lax.all_to_all(field, "vec", split_axis=1, concat_axis=0, tiled=True)
    all_vectors = regrouped.shape[0]
    total_cells = levels * lax.axis_size("tiles") * tile_rows * tile_cols
    flat_values = regrouped.reshape(all_vectors, -1)
    weighted = (regrouped * volume[None, None]).reshape(all_vectors, -1)
    gram_local = (
        lax.dot_general(
            weighted,
            flat_values,
            (((1,), (1,)), ((), ())),
            precision=lax.Precision.HIGHEST,
            preferred_element_type=jnp.float32,
        )
        / total_cells
    )
    gram = lax.psum(gram_local, ("tiles", "vec"))
    r_factor = jnp.linalg.cholesky(gram).T
    return (field, r_factor)


def solution(mesh):
    in_specs = (
        P("vec", None, "tiles", None),
        P(None, None, "tiles", None),
        P("tiles", None),
        P("tiles", None),
        P("tiles", None),
    )
    out_specs = (P("vec", None, "tiles", None), P())
    return jax.shard_map(shards, mesh=mesh, in_specs=in_specs, out_specs=out_specs, check_vma=False)
```

profile of v0, /device:TPU:0, one launch (start us, length us, event | category | flops | bytes accessed | tf_op | source)
XLA Modules:
  0.0 360.7 jit_solution(15413979670254158427)
XLA Ops:
  7.2 1.5 fusion.34
  14.1 5.9 %collective-permute-start = (f32[4,4,1,128]{3,2,1,0:T(1,128)S(1)}, f32[4,4,1,128]{3,2,1,0:T(1,128)S(1)}, u32[]{:S(2)}, u32[]{:S(2)}) collective-permute-start(f32[4,4,1,128]{3,2,1,0:T(1,128)S(1)} %get-tuple-element.29), channel_id=1, source_target_pairs={{0,16},{2,18},{4,20},{6,22},{8,24},{10,26},{12,28},{14,30},{16,32}... | collective-permute-start | bytes 24584 | tf_op jit(solution)/shard_map/ppermute | solution.py:13
  21.3 1.8 copy_multiply_fusion
  23.1 3.9 %collective-permute-done.1 = f32[4,4,1,128]{3,2,1,0:T(1,128)S(1)} collective-permute-done((f32[4,4,1,128]{3,2,1,0:T(1,128)S(1)}, f32[4,4,1,128]{3,2,1,0:T(1,128)S(1)}, u32[]{:S(2)}, u32[]{:S(2)}) %collective-permute-start.1) | collective-permute-done | bytes 8224 | tf_op jit(solution)/shard_map/ppermute | solution.py:13
  27.2 1.3 collective-permute-start.2
  29.8 10.1 %collective-permute-start.4 = (f32[64,4,1,128]{3,0,2,1:T(8,128)S(1)}, f32[64,4,1,128]{3,0,2,1:T(8,128)S(1)}, u32[]{:S(2)}, u32[]{:S(2)}) collective-permute-start(f32[64,4,1,128]{3,0,2,1:T(8,128)S(1)} %get-tuple-element.22), channel_id=1, source_target_pairs={{0,16},{2,18},{4,20},{6,22},{8,24},{10,26},{12,28},{14,30},{16,32}... | collective-permute-start | bytes 393224 | tf_op jit(solution)/shard_map/ppermute | solution.py:13
  41.5 2.3 collective-permute-done.4
  43.8 4.8 %collective-permute-done.5 = f32[64,4,1,128]{3,0,2,1:T(8,128)S(1)} collective-permute-done((f32[64,4,1,128]{3,0,2,1:T(8,128)S(1)}, f32[64,4,1,128]{3,0,2,1:T(8,128)S(1)}, u32[]{:S(2)}, u32[]{:S(2)}) %collective-permute-start.5) | collective-permute-done | bytes 131104 | tf_op jit(solution)/shard_map/ppermute | solution.py:13
  48.7 1.5 fusion.28
  50.2 2.0 copy.15
  52.9 1.3 collective-permute-start.7
  54.2 3.0 collective-permute-start.6
  58.6 1.6 copy.18
  60.2 2.4 pad_maximum_fusion
  65.5 1.3 fusion.23
  66.8 11.9 %collective-permute-start.8 = (f32[64,4,1,128]{3,0,2,1:T(8,128)S(1)}, f32[64,4,1,128]{3,0,2,1:T(8,128)S(1)}, u32[]{:S(2)}, u32[]{:S(2)}) collective-permute-start(f32[64,4,1,128]{3,0,2,1:T(8,128)S(1)} %get-tuple-element.20), channel_id=1, source_target_pairs={{0,16},{2,18},{4,20},{6,22},{8,24},{10,26},{12,28},{14,30},{16,32}... | collective-permute-start | bytes 393224 | tf_op jit(solution)/shard_map/ppermute | solution.py:13
  81.2 5.9 %collective-permute-done.9 = f32[64,4,1,128]{3,0,2,1:T(8,128)S(1)} collective-permute-done((f32[64,4,1,128]{3,0,2,1:T(8,128)S(1)}, f32[64,4,1,128]{3,0,2,1:T(8,128)S(1)}, u32[]{:S(2)}, u32[]{:S(2)}) %collective-permute-start.9) | collective-permute-done | bytes 131104 | tf_op jit(solution)/shard_map/ppermute | solution.py:13
  87.2 1.5 fusion.27
  88.7 2.0 copy.21
  90.7 1.3 collective-permute-start.10
  92.7 1.5 collective-permute-start.11
  95.8 1.6 copy.24
  97.4 2.4 pad_maximum_fusion.1
  102.3 1.3 fusion.20
  103.6 10.5 %collective-permute-start.12 = (f32[64,4,1,128]{3,0,2,1:T(8,128)S(1)}, f32[64,4,1,128]{3,0,2,1:T(8,128)S(1)}, u32[]{:S(2)}, u32[]{:S(2)}) collective-permute-start(f32[64,4,1,128]{3,0,2,1:T(8,128)S(1)} %get-tuple-element.18), channel_id=1, source_target_pairs={{0,16},{2,18},{4,20},{6,22},{8,24},{10,26},{12,28},{14,30},{16,32}... | collective-permute-start | bytes 393224 | tf_op jit(solution)/shard_map/ppermute | solution.py:13
  116.7 5.9 %collective-permute-done.13 = f32[64,4,1,128]{3,0,2,1:T(8,128)S(1)} collective-permute-done((f32[64,4,1,128]{3,0,2,1:T(8,128)S(1)}, f32[64,4,1,128]{3,0,2,1:T(8,128)S(1)}, u32[]{:S(2)}, u32[]{:S(2)}) %collective-permute-start.13) | collective-permute-done | bytes 131104 | tf_op jit(solution)/shard_map/ppermute | solution.py:13
  122.6 1.5 fusion.26
  124.2 2.0 copy.27
  126.2 1.3 collective-permute-start.14
  128.2 1.3 collective-permute-start.15
  129.9 1.3 collective-permute-done.15
  131.3 1.6 copy.30
  132.8 2.4 pad_maximum_fusion.2
  137.7 1.3 fusion.17
  139.1 12.4 %collective-permute-start.16 = (f32[64,4,1,128]{3,0,2,1:T(8,128)S(1)}, f32[64,4,1,128]{3,0,2,1:T(8,128)S(1)}, u32[]{:S(2)}, u32[]{:S(2)}) collective-permute-start(f32[64,4,1,128]{3,0,2,1:T(8,128)S(1)} %get-tuple-element.16), channel_id=1, source_target_pairs={{0,16},{2,18},{4,20},{6,22},{8,24},{10,26},{12,28},{14,30},{16,32}... | collective-permute-start | bytes 393224 | tf_op jit(solution)/shard_map/ppermute | solution.py:13
  154.0 5.9 %collective-permute-done.17 = f32[64,4,1,128]{3,0,2,1:T(8,128)S(1)} collective-permute-done((f32[64,4,1,128]{3,0,2,1:T(8,128)S(1)}, f32[64,4,1,128]{3,0,2,1:T(8,128)S(1)}, u32[]{:S(2)}, u32[]{:S(2)}) %collective-permute-start.17) | collective-permute-done | bytes 131104 | tf_op jit(solution)/shard_map/ppermute | solution.py:13
  159.9 1.5 fusion.25
  161.5 2.0 copy.33
  165.4 1.5 collective-permute-start.19
  168.5 1.6 copy.36
  170.1 2.4 pad_maximum_fusion.3
  175.0 1.3 fusion.14
  177.0 16.7 %all_to_all.15 = f32[64,4,8,128]{3,2,0,1:T(8,128)S(1)} all-to-all(f32[64,4,8,128]{3,2,0,1:T(8,128)S(1)} %copy.39), channel_id=1, replica_groups=mesh['tiles'=64,'vec'=2] {'vec'}, dimensions={1} | all-to-all | bytes 2097152 | tf_op jit(solution)/shard_map/all_to_all | solution.py:80
  194.8 1.4 reshape.96
  197.3 2.9 convolution_multiply_fusion
  200.2 1.6 copy.43
  201.7 136.5 %all-reduce.10.cloned.1.call-done = f32[128,128]{0,1:T(8,128)} async-done(((f32[128,128]{0,1:T(8,128)}), f32[128,128]{0,1:T(8,128)}) %all-reduce.10.cloned.1.call-update) | async-done | bytes 65552 | tf_op jit(solution)/shard_map/psum | solution.py:95
  340.0 11.7 %cholesky.18 = f32[128,128]{1,0:T(8,128)S(1)} custom-call(f32[128,128]{1,0:T(8,128)S(1)} %fusion.24), custom_call_target="Cholesky" | custom-call | tf_op jit(solution)/shard_map/jit(cholesky)/cholesky | solution.py:96
  (96 shorter events, 41.0 us)
Async XLA Ops:
  7.2 331.1 %all-reduce.10.cloned.1.call-start = ((), (), s32[]{:S(2)}) async-start(), calls=%async_computation.1 | async-start | bytes 131072 | tf_op jit(solution)/shard_map/psum | solution.py:95
  14.1 9.0 %collective-permute-start = (f32[4,4,1,128]{3,2,1,0:T(1,128)S(1)}, f32[4,4,1,128]{3,2,1,0:T(1,128)S(1)}, u32[]{:S(2)}, u32[]{:S(2)}) collective-permute-start(f32[4,4,1,128]{3,2,1,0:T(1,128)S(1)} %get-tuple-element.29), channel_id=1, source_target_pairs={{0,16},{2,18},{4,20},{6,22},{8,24},{10,26},{12,28},{14,30},{16,32}... | collective-permute-start | bytes 24584 | tf_op jit(solution)/shard_map/ppermute | solution.py:13
  20.0 7.0 %collective-permute-start.1 = (f32[4,4,1,128]{3,2,1,0:T(1,128)S(1)}, f32[4,4,1,128]{3,2,1,0:T(1,128)S(1)}, u32[]{:S(2)}, u32[]{:S(2)}) collective-permute-start(f32[4,4,1,128]{3,2,1,0:T(1,128)S(1)} %get-tuple-element.30), channel_id=1, source_target_pairs={{16,0},{18,2},{20,4},{22,6},{24,8},{26,10},{28,12},{30,14},{32,16}... | collective-permute-start | bytes 24584 | tf_op jit(solution)/shard_map/ppermute | solution.py:13
  27.2 14.0 %collective-permute-start.2 = (f32[4,4,10,1]{3,2,1,0:T(8,128)S(1)}, f32[4,4,10,1]{3,2,1,0:T(8,128)S(1)}, u32[]{:S(2)}, u32[]{:S(2)}) collective-permute-start(f32[4,4,10,1]{3,2,1,0:T(8,128)S(1)} %get-tuple-element.27), channel_id=1, source_target_pairs={{0,2},{2,4},{4,6},{6,8},{8,10},{10,12},{12,14},{14,16},{16,18},{18... | collective-permute-start | bytes 1928 | tf_op jit(solution)/shard_map/ppermute | solution.py:13
  28.5 12.7 %collective-permute-start.3 = (f32[4,4,10,1]{3,2,1,0:T(8,128)S(1)}, f32[4,4,10,1]{3,2,1,0:T(8,128)S(1)}, u32[]{:S(2)}, u32[]{:S(2)}) collective-permute-start(f32[4,4,10,1]{3,2,1,0:T(8,128)S(1)} %get-tuple-element.28), channel_id=1, source_target_pairs={{2,0},{4,2},{6,4},{8,6},{10,8},{12,10},{14,12},{16,14},{18,16},{20... | collective-permute-start | bytes 1928 | tf_op jit(solution)/shard_map/ppermute | solution.py:13
  29.8 14.0 %collective-permute-start.4 = (f32[64,4,1,128]{3,0,2,1:T(8,128)S(1)}, f32[64,4,1,128]{3,0,2,1:T(8,128)S(1)}, u32[]{:S(2)}, u32[]{:S(2)}) collective-permute-start(f32[64,4,1,128]{3,0,2,1:T(8,128)S(1)} %get-tuple-element.22), channel_id=1, source_target_pairs={{0,16},{2,18},{4,20},{6,22},{8,24},{10,26},{12,28},{14,30},{16,32}... | collective-permute-start | bytes 393224 | tf_op jit(solution)/shard_map/ppermute | solution.py:13
  39.9 8.7 %collective-permute-start.5 = (f32[64,4,1,128]{3,0,2,1:T(8,128)S(1)}, f32[64,4,1,128]{3,0,2,1:T(8,128)S(1)}, u32[]{:S(2)}, u32[]{:S(2)}) collective-permute-start(f32[64,4,1,128]{3,0,2,1:T(8,128)S(1)} %get-tuple-element.23), channel_id=1, source_target_pairs={{16,0},{18,2},{20,4},{22,6},{24,8},{26,10},{28,12},{30,14},{32,16}... | collective-permute-start | bytes 393224 | tf_op jit(solution)/shard_map/ppermute | solution.py:13
  52.9 5.7 %collective-permute-start.7 = (f32[64,4,10,1]{0,2,3,1:T(8,128)S(1)}, f32[64,4,10,1]{0,2,3,1:T(8,128)S(1)}, u32[]{:S(2)}, u32[]{:S(2)}) collective-permute-start(f32[64,4,10,1]{0,2,3,1:T(8,128)S(1)} %copy.16), channel_id=1, source_target_pairs={{2,0},{4,2},{6,4},{8,6},{10,8},{12,10},{14,12},{16,14},{18,16},{20... | collective-permute-start | bytes 30728 | tf_op jit(solution)/shard_map/ppermute | solution.py:13
  54.2 3.9 %collective-permute-start.6 = (f32[64,4,10,1]{0,2,3,1:T(8,128)S(1)}, f32[64,4,10,1]{0,2,3,1:T(8,128)S(1)}, u32[]{:S(2)}, u32[]{:S(2)}) collective-permute-start(f32[64,4,10,1]{0,2,3,1:T(8,128)S(1)} %copy.15), channel_id=1, source_target_pairs={{0,2},{2,4},{4,6},{6,8},{8,10},{10,12},{12,14},{14,16},{16,18},{18... | collective-permute-start | bytes 30728 | tf_op jit(solution)/shard_map/ppermute | solution.py:13
  57.3 42.5 %copy-start.5 = (f32[3,10,130]{2,1,0:T(8,128)}, f32[3,10,130]{2,1,0:T(8,128)S(1)}, u32[]{:S(2)}) copy-start(f32[3,10,130]{2,1,0:T(8,128)S(1)} %slice_bitcast_fusion.3) | copy-start | bytes 46804
  62.9 1.3 copy-start.1
  64.2 1.2 copy-start.4
  66.8 14.4 %collective-permute-start.8 = (f32[64,4,1,128]{3,0,2,1:T(8,128)S(1)}, f32[64,4,1,128]{3,0,2,1:T(8,128)S(1)}, u32[]{:S(2)}, u32[]{:S(2)}) collective-permute-start(f32[64,4,1,128]{3,0,2,1:T(8,128)S(1)} %get-tuple-element.20), channel_id=1, source_target_pairs={{0,16},{2,18},{4,20},{6,22},{8,24},{10,26},{12,28},{14,30},{16,32}... | collective-permute-start | bytes 393224 | tf_op jit(solution)/shard_map/ppermute | solution.py:13
  78.7 8.4 %collective-permute-start.9 = (f32[64,4,1,128]{3,0,2,1:T(8,128)S(1)}, f32[64,4,1,128]{3,0,2,1:T(8,128)S(1)}, u32[]{:S(2)}, u32[]{:S(2)}) collective-permute-start(f32[64,4,1,128]{3,0,2,1:T(8,128)S(1)} %get-tuple-element.21), channel_id=1, source_target_pairs={{16,0},{18,2},{20,4},{22,6},{24,8},{26,10},{28,12},{30,14},{32,16}... | collective-permute-start | bytes 393224 | tf_op jit(solution)/shard_map/ppermute | solution.py:13
  90.7 3.5 collective-permute-start.10
  92.7 3.1 collective-permute-start.11
  100.2 1.3 copy-start.2
  103.6 13.0 %collective-permute-start.12 = (f32[64,4,1,128]{3,0,2,1:T(8,128)S(1)}, f32[64,4,1,128]{3,0,2,1:T(8,128)S(1)}, u32[]{:S(2)}, u32[]{:S(2)}) collective-permute-start(f32[64,4,1,128]{3,0,2,1:T(8,128)S(1)} %get-tuple-element.18), channel_id=1, source_target_pairs={{0,16},{2,18},{4,20},{6,22},{8,24},{10,26},{12,28},{14,30},{16,32}... | collective-permute-start | bytes 393224 | tf_op jit(solution)/shard_map/ppermute | solution.py:13
  114.2 8.4 %collective-permute-start.13 = (f32[64,4,1,128]{3,0,2,1:T(8,128)S(1)}, f32[64,4,1,128]{3,0,2,1:T(8,128)S(1)}, u32[]{:S(2)}, u32[]{:S(2)}) collective-permute-start(f32[64,4,1,128]{3,0,2,1:T(8,128)S(1)} %get-tuple-element.19), channel_id=1, source_target_pairs={{16,0},{18,2},{20,4},{22,6},{24,8},{26,10},{28,12},{30,14},{32,16}... | collective-permute-start | bytes 393224 | tf_op jit(solution)/shard_map/ppermute | solution.py:13
  126.2 3.3 collective-permute-start.14
  128.2 3.1 collective-permute-start.15
  132.8 2.4 copy-start.6
  135.6 1.3 copy-start.3
  139.1 14.9 %collective-permute-start.16 = (f32[64,4,1,128]{3,0,2,1:T(8,128)S(1)}, f32[64,4,1,128]{3,0,2,1:T(8,128)S(1)}, u32[]{:S(2)}, u32[]{:S(2)}) collective-permute-start(f32[64,4,1,128]{3,0,2,1:T(8,128)S(1)} %get-tuple-element.16), channel_id=1, source_target_pairs={{0,16},{2,18},{4,20},{6,22},{8,24},{10,26},{12,28},{14,30},{16,32}... | collective-permute-start | bytes 393224 | tf_op jit(solution)/shard_map/ppermute | solution.py:13
  151.5 8.4 %collective-permute-start.17 = (f32[64,4,1,128]{3,0,2,1:T(8,128)S(1)}, f32[64,4,1,128]{3,0,2,1:T(8,128)S(1)}, u32[]{:S(2)}, u32[]{:S(2)}) collective-permute-start(f32[64,4,1,128]{3,0,2,1:T(8,128)S(1)} %get-tuple-element.17), channel_id=1, source_target_pairs={{16,0},{18,2},{20,4},{22,6},{24,8},{26,10},{28,12},{30,14},{32,16}... | collective-permute-start | bytes 393224 | tf_op jit(solution)/shard_map/ppermute | solution.py:13
  163.5 3.5 collective-permute-start.18
  165.4 3.1 collective-permute-start.19
  170.1 2.4 copy-start.7
  172.9 1.3 copy-start
  176.9 17.7 %copy-start.8 = (f32[8,128]{1,0:T(8,128)S(1)}, f32[8,128]{1,0:T(8,128)}, u32[]{:S(2)}) copy-start(f32[8,128]{1,0:T(8,128)} %param.8) | copy-start | bytes 12292
Sparse Core Ops, SparseCore 0:
  200.3 137.9 all-reduce.9
where the time goes:
time: 365 us; the launch traced here: 361 us
  waiting for transfers between devices  173 us (47%)
  starting transfers between devices  72.4 us (20%)
  other arithmetic  40.4 us (11%)
  local copies, waits for them, and re-layouts  38.2 us (10%)
  between operations  17.2 us (5%)
  blocking collectives  16.7 us (5%)
    psum x1, waiting for transfers between devices, shards(): gram = lax.psum(gram_local, ('tiles', 'vec'))  137 us
    ppermute x20, starting transfers between devices, shifted(): lax.ppermute(value, axis, [(source, source + steps) for source in range(f...  72.3 us
    ppermute x20, waiting for transfers between devices, shifted(): lax.ppermute(value, axis, [(source, source + steps) for source in range(f...  36.4 us
    all_to_all x1, blocking collectives, shards(): lax.all_to_all(field, 'vec', split_axis=1, concat_axis=0, tiled=True)  16.7 us
    slice x9, local copies, waits for them, and re-layouts, extend(): left_rim = neighbour(stacked[:, :, :, -margin:], 1)  14.2 us
    another operation x3, other arithmetic, shards(): r_factor = jnp.linalg.cholesky(gram).T  12.4 us
    concatenate x5, other arithmetic, extend(): return jnp.concatenate([left_rim, stacked, right_rim], axis=3)  9.82 us
    ppermute x8, local copies, waits for them, and re-layouts, shifted(): lax.ppermute(value, axis, [(source, source + steps) for source in range(f...  8.08 us
  transfers between devices with their start and end apart: 21, of which 14 were waited for; matrix products, arithmetic and copies ran while one was open for 2% of the time, Pallas kernels for 0%

commit v1 on v0

v1 whole, which is shorter than its diff:
```python
import functools
import jax
import jax.numpy as jnp
from jax import lax
from jax.sharding import PartitionSpec as P
from jax.experimental import pallas as pl
from jax.experimental.pallas import tpu as pltpu

MESH = pl.DeviceIdType.MESH
F32 = jnp.float32
LEV = 4
NG = 8
NCOEF = 7
CELLS = 4 * 512 * 128
HIGH = lax.Precision.HIGHEST


def did(t, v):
    return {"tiles": t, "vec": v}


def nt_dot(a, b):
    return lax.dot_general(a, b, (((1,), (1,)), ((), ())), precision=HIGH, preferred_element_type=F32)


def kernel(
    om, cond, wet, vol, runs,
    out, gram,
    om_v, halo, cond_v, wet_v, vol_v, runs_s,
    xm, xl, xr, cf, cbm, cbe,
    up_own, u_l, u_r, u_lr, u_h,
    buf_a, buf_b, fin, part, out_v,
    red_c, red_x, red_y, red_z,
    lsem, osem, hs, hr, ss, sr, es, er, us, ur, fs, fr, vs, vr, cs, cr, xs, xrs, ys, yr, zs, zr,
):
    t = lax.axis_index("tiles")
    v = lax.axis_index("vec")
    w = 1 - v
    core = lax.rem(t, 2)
    px = lax.rem(t // 2, 4)
    zh = lax.rem(t // 8, 2)
    py = t // 16
    tcol = lax.rem(t, 8)
    base = t - tcol
    up = lax.rem(t + 56, 64)
    down = lax.rem(t + 8, 64)
    left = base + lax.rem(tcol + 7, 8)
    right = base + lax.rem(tcol + 1, 8)
    pair = t + 1 - 2 * core
    zpair = t + 8 - 16 * zh
    x_peers = [t - 2 * px + 2 * lax.rem(px + d, 4) for d in (1, 2, 3)]
    y_peers = [t - 16 * py + 16 * lax.rem(py + d, 4) for d in (1, 2, 3)]

    loads = [
        pltpu.make_async_copy(cond, cond_v, lsem.at[0]),
        pltpu.make_async_copy(wet, wet_v, lsem.at[1]),
        pltpu.make_async_copy(runs, runs_s, lsem.at[2]),
        pltpu.make_async_copy(vol, vol_v, lsem.at[3]),
        pltpu.make_async_copy(om, om_v, lsem.at[4]),
    ]
    for cp in loads:
        cp.start()

    barrier = pltpu.get_barrier_semaphore()
    greet = [(up, v), (down, v), (left, v), (right, v)]
    greet += [(p, v) for p in x_peers] + [(p, v) for p in y_peers]
    greet += [(t, w), (zpair, w)]
    for p in greet:
        pl.semaphore_signal(barrier, inc=1, device_id=did(*p), device_id_type=MESH)

    for cp in loads[:3]:
        cp.wait()
    rows = lax.broadcasted_iota(jnp.int32, (8, 128), 0)
    cols = lax.broadcasted_iota(jnp.int32, (8, 128), 1)
    r0, r1, r2, r3 = (runs_s[0, k] for k in range(4))
    closed_x = (rows == 0) & ((cols < r0) | (cols >= r0 + r1))
    closed_y = (cols == 0) & ((rows < r2) | (rows >= r2 + r3))
    own = pl.ds(4, 8)
    for l in range(LEV):
        xm[l, own, :] = jnp.where(closed_x, 0.0, cond_v[0, l])
        xm[4 + l, own, :] = jnp.where(closed_y, 0.0, cond_v[1, l])
        xm[8 + l, own, :] = cond_v[2, l] if l else jnp.zeros((8, 128), F32)
    xm[12, own, :] = wet_v[...].astype(F32)

    pl.semaphore_wait(barrier, len(greet))

    def remote(src, dst, s, r, to):
        return pltpu.make_async_remote_copy(
            src_ref=src, dst_ref=dst, send_sem=s, recv_sem=r, device_id=did(*to), device_id_type=MESH
        )

    stat = [
        remote(xm.at[:, pl.ds(4, 4), :], xm.at[:, pl.ds(12, 4), :], ss.at[0], sr.at[0], (up, v)),
        remote(xm.at[:, pl.ds(8, 4), :], xm.at[:, pl.ds(0, 4), :], ss.at[1], sr.at[1], (down, v)),
    ]
    for cp in stat:
        cp.start()

    def halo_copy(g, d):
        blk = pl.ds(g * 32, 32)
        half = pl.ds(4 * d, 4)
        return remote(
            om.at[blk, half, :], halo.at[blk, half, :], hs.at[g, d], hr.at[g, d], (down if d else up, v)
        )

    for g in range(NG):
        for d in range(2):
            halo_copy(g, d).start()

    for cp in loads[3:]:
        cp.wait()
    om2 = om_v.reshape(2048, 128)
    halo2 = halo.reshape(2048, 128)
    out2 = out_v.reshape(2048, 128)

    def pack(g, c):
        for h in range(2):
            acc = jnp.zeros((8, 128), F32)
            for k in range(16):
                row = (k // 4) * 8 + 4 * h + k % 4
                val = om2[pl.ds(g * 256 + row, 8, stride=32), :]
                acc = jnp.where(cols // 8 == k, pltpu.roll(val, (k * 8 + 4) % 128, 1), acc)
            up_own[h, g] = acc
        return c

    lax.fori_loop(0, NG, pack, 0)
    edges = [
        remote(up_own, u_r, es.at[0], er.at[0], (left, v)),
        remote(up_own, u_l, es.at[1], er.at[1], (right, v)),
    ]
    for cp in edges:
        cp.start()

    for cp in stat:
        cp.wait_recv()
    stat_e = [
        remote(xm, xr, ss.at[2], sr.at[2], (left, v)),
        remote(xm, xl, ss.at[3], sr.at[3], (right, v)),
    ]
    for cp in stat_e:
        cp.start()

    for cp in edges:
        cp.wait_recv()

    def merge(g, c):
        for h in range(2):
            u_lr[h, g] = jnp.where(cols % 8 < 4, u_l[h, g], u_r[h, g])
        return c

    lax.fori_loop(0, NG, merge, 0)
    fwd = [
        remote(u_lr.at[0], u_h.at[0], us.at[0], ur.at[0], (up, v)),
        remote(u_lr.at[1], u_h.at[1], us.at[1], ur.at[1], (down, v)),
    ]
    for cp in fwd:
        cp.start()

    for cp in stat_e:
        cp.wait_recv()

    lanes = lax.broadcasted_iota(jnp.int32, (16, 128), 1)

    def both(k):
        return xm[k], jnp.where(lanes < 64, xr[k], xl[k])

    wets = both(12)
    for l in range(LEV):
        cxs, cys, czs = both(l), both(4 + l), both(8 + l)
        cps = both(9 + l) if l < 3 else (jnp.zeros((16, 128), F32),) * 2
        for e in range(2):
            cx, cy, cz, cp, wt = cxs[e], cys[e], czs[e], cps[e], wets[e]
            cxn = pltpu.roll(cx, 15, 0)
            cyn = pltpu.roll(jnp.where(lanes == 0, cys[1 - e], cy), 127, 1)
            total = cx + cxn + cy + cyn + cz + cp
            for k, val in enumerate((1.0 - total, cx, cxn, cy, cyn, cz, cp)):
                cf[e, l * NCOEF + k] = wt * val
    for e in range(2):
        cf[e, LEV * NCOEF] = wets[e]

    def spread(r, c):
        for e, dst in ((0, cbm), (1, cbe)):
            for k in range(LEV * NCOEF + 1):
                dst[r, k] = jnp.broadcast_to(cf[e, k, pl.ds(r, 1), :], (8, 128))
        return c

    lax.fori_loop(0, 16, spread, 0)
    for cp in fwd:
        cp.wait_recv()

    last = cols == 127
    first = cols == 0

    def vec_copy(g):
        grp = pl.ds(pl.multiple_of(g * 8, 8), 8)
        return remote(fin.at[pl.ds(w * 16, 16), grp, :], part.at[:, grp, :], vs.at[g], vr.at[g], (t, w))

    def out_copy(g):
        blk = pl.ds(g * 32, 32)
        return pltpu.make_async_copy(out_v.at[blk], out.at[blk], osem.at[g])

    def group(g, c):
        for d in range(2):
            halo_copy(g, d).wait_recv()
        for r in range(16):
            own_row = 4 <= r < 12
            hr_ = (r - 4) if own_row else (r + 4 if r < 4 else r - 12)
            src = om2 if own_row else halo2
            upk = u_lr if own_row else u_h
            wm = cbm[r, LEV * NCOEF]
            we = cbe[r, LEV * NCOEF]
            pk = upk[hr_ // 4, g]
            for l in range(LEV):
                k = l * 4 + hr_ % 4
                buf_a[r, 2 * l] = wm * src[pl.ds(g * 256 + l * 8 + hr_, 8, stride=32), :]
                buf_a[r, 2 * l + 1] = we * pltpu.roll(pk, (256 - (k * 8 + 4)) % 128, 1)
        bufs = (buf_a, buf_b)
        for p in range(4):
            src, dst = bufs[p % 2], bufs[(p + 1) % 2]

            def one_row(r, c, src=src, dst=dst, final=(p == 3)):
                mid = [[src[r, 2 * l + e] for e in range(2)] for l in range(LEV)]
                for l in range(LEV):
                    for e in range(1 if final else 2):
                        cb = cbe if e else cbm
                        me, other = mid[l][e], mid[l][1 - e]
                        f_l = pltpu.roll(jnp.where(last, other, me), 1, 1)
                        f_r = pltpu.roll(jnp.where(first, other, me), 127, 1)
                        k = l * NCOEF
                        acc = cb[r, k] * me
                        acc += cb[r, k + 1] * src[r - 1, 2 * l + e]
                        acc += cb[r, k + 2] * src[r + 1, 2 * l + e]
                        acc += cb[r, k + 3] * f_l
                        acc += cb[r, k + 4] * f_r
                        if l > 0:
                            acc += cb[r, k + 5] * mid[l - 1][e]
                        if l < 3:
                            acc += cb[r, k + 6] * mid[l + 1][e]
                        if final:
                            fin[l * 8 + r - 4, pl.ds(pl.multiple_of(g * 8, 8), 8), :] = acc
                            out2[pl.ds(g * 256 + l * 8 + r - 4, 8, stride=32), :] = acc
                        else:
                            dst[r, 2 * l + e] = acc
                return c

            lax.fori_loop(1 + p, 15 - p, one_row, 0)
        vec_copy(g).start()
        out_copy(g).start()
        return c

    lax.fori_loop(0, NG, group, 0)

    def own_block(i, acc):
        a = fin[i]
        return acc + nt_dot(a * vol_v[pl.ds(lax.rem(i, 8), 1), :], a)

    g_own = lax.fori_loop(0, 32, own_block, jnp.zeros((64, 64), F32))
    for g in range(NG):
        vec_copy(g).wait_recv()

    def cross_block(i, acc):
        mine, theirs = fin[v * 16 + i], part[i]
        a = jnp.where(v == 0, mine, theirs)
        b = jnp.where(v == 0, theirs, mine)
        return acc + nt_dot(a * vol_v[pl.ds(lax.rem(i, 8), 1), :], b)

    g_cross = lax.fori_loop(0, 16, cross_block, jnp.zeros((64, 64), F32))

    def stage(val, red, slot, peers, s, r):
        red[slot] = val
        cps = [remote(red.at[slot], red.at[slot], s.at[j], r.at[j], p) for j, p in enumerate(peers)]
        for cp in cps:
            cp.start()
        for cp in cps:
            cp.wait_recv()
        return cps

    sent = []
    val = jnp.concatenate([g_own, g_cross], axis=1)
    sent += stage(val, red_c, core, [(pair, v)], cs, cr)
    val = red_c[0] + red_c[1]
    sent += stage(val, red_x, px, [(p, v) for p in x_peers], xs, xrs)
    val = (red_x[0] + red_x[1]) + (red_x[2] + red_x[3])
    sent += stage(val, red_y, py, [(p, v) for p in y_peers], ys, yr)
    val = (red_y[0] + red_y[1]) + (red_y[2] + red_y[3])
    sent += stage(val, red_z, 2 * zh + v, [(t, w), (zpair, v), (zpair, w)], zs, zr)
    scale = 1.0 / CELLS
    even = red_z[0] + red_z[2]
    odd = red_z[1] + red_z[3]
    g00 = even[:, :64] * scale
    g11 = odd[:, :64] * scale
    g01 = (even[:, 64:] + odd[:, 64:]) * scale
    gram[pl.ds(0, 64), :] = jnp.concatenate([g00, g01], axis=1)
    gram[pl.ds(64, 64), :] = jnp.concatenate([g01.T, g11], axis=1)

    for cp in sent + stat + stat_e + edges + fwd:
        cp.wait_send()
    for g in range(NG):
        for d in range(2):
            halo_copy(g, d).wait_send()
        vec_copy(g).wait_send()
        out_copy(g).wait()


def shards(omega, conductance, wet, volume, face_runs):
    vm = lambda *s: pltpu.VMEM(s, F32)
    dma = lambda *s: pltpu.SemaphoreType.DMA(s)
    scratch = [
        vm(256, 8, 128), vm(256, 8, 128), vm(3, 4, 8, 128), pltpu.VMEM((8, 128), jnp.int32), vm(8, 128),
        pltpu.SMEM((1, 4), jnp.int32),
        vm(13, 16, 128), vm(13, 16, 128), vm(13, 16, 128), vm(2, 29, 16, 128),
        vm(16, 29, 8, 128), vm(16, 29, 8, 128),
        vm(2, 8, 8, 128), vm(2, 8, 8, 128), vm(2, 8, 8, 128), vm(2, 8, 8, 128), vm(2, 8, 8, 128),
        vm(16, 8, 8, 128), vm(16, 8, 8, 128), vm(32, 64, 128), vm(16, 64, 128), vm(256, 8, 128),
        vm(2, 64, 128), vm(4, 64, 128), vm(4, 64, 128), vm(4, 64, 128),
        dma(5), dma(8), dma(8, 2), dma(8, 2), dma(4), dma(4), dma(2), dma(2), dma(2), dma(2),
        dma(2), dma(2), dma(8), dma(8), dma(1), dma(1), dma(3), dma(3), dma(3), dma(3), dma(3), dma(3),
    ]
    anys = pl.BlockSpec(memory_space=pl.ANY)
    diffused, gram = pl.pallas_call(
        kernel,
        out_shape=(jax.ShapeDtypeStruct((256, 8, 128), F32), jax.ShapeDtypeStruct((128, 128), F32)),
        in_specs=[anys] * 5,
        out_specs=(anys, pl.BlockSpec(memory_space=pltpu.VMEM)),
        scratch_shapes=scratch,
        compiler_params=pltpu.CompilerParams(
            collective_id=0, has_side_effects=True, vmem_limit_bytes=48 * 1024 * 1024
        ),
        name="range_finder",
    )(omega.reshape(256, 8, 128), conductance, wet, volume, face_runs)
    r_factor = lax.linalg.cholesky(gram, symmetrize_input=False).T
    return (diffused.reshape(omega.shape), r_factor)


def solution(mesh):
    in_specs = (
        P("vec", None, "tiles", None),
        P(None, None, "tiles", None),
        P("tiles", None),
        P("tiles", None),
        P("tiles", None),
    )
    out_specs = (P("vec", None, "tiles", None), P())
    return jax.shard_map(shards, mesh=mesh, in_specs=in_specs, out_specs=out_specs, check_vma=False)
```

time: 365 us -> 112 us (0.31); the launches traced: 361 us -> 112 us
  waiting for transfers between devices: 173 us -> 0 us
  Pallas kernels: 0 us -> 92.5 us
  starting transfers between devices: 72.4 us -> 0 us
  local copies, waits for them, and re-layouts: 38.2 us -> 5.74 us
  other arithmetic: 40.4 us -> 13 us
  blocking collectives: 16.7 us -> 0 us
  between operations: 17.2 us -> 0.66 us
    psum x1 -> x0, waiting for transfers between devices: 137 us -> none  [shards(): gram = lax.psum(gram_local, ('tiles', 'vec'))]
    pallas_call x0 -> x1, Pallas kernels: none -> 92.5 us  [shards(): pl.pallas_call(kernel, out_shape=(jax.ShapeDtypeStruct((256, 8, 128), F32...]
    ppermute x20 -> x0, starting transfers between devices: 72.3 us -> none  [shifted(): lax.ppermute(value, axis, [(source, source + steps) for source in range(f...]
    ppermute x20 -> x0, waiting for transfers between devices: 36.4 us -> none  [shifted(): lax.ppermute(value, axis, [(source, source + steps) for source in range(f...]
    slice x21 -> x0, local copies, waits for them, and re-layouts: 18.7 us -> none  [the longest x9 14.2 us: extend(): left_rim = neighbour(stacked[:, :, :, -margin:], 1)]
    all_to_all x1 -> x0, blocking collectives: 16.7 us -> none  [shards(): lax.all_to_all(field, 'vec', split_axis=1, concat_axis=0, tiled=True)]
    mul x19 -> x0, other arithmetic: 14.3 us -> none  [the longest x4 5.28 us: diffuse(): return wet_cells[:, 1:-1, 1:-1] * (field[:, :, 1:-1, 1:-1] + change)]
    concatenate x10 -> x0, other arithmetic: 10.2 us -> none  [the longest x5 9.82 us: extend(): return jnp.concatenate([left_rim, stacked, right_rim], axis=3)]
  transfers between devices with their start and end apart: 21 -> 0, of which waited for: 14 -> 0; matrix products, arithmetic and copies ran while one was open for 2% -> 0% of each run, Pallas kernels for 0% -> 0%
where the time goes in v1:
time: 112 us
  Pallas kernels  92.5 us (83%)
  other arithmetic  13 us (12%)
  local copies, waits for them, and re-layouts  5.74 us (5%)
    pallas_call x1, Pallas kernels, shards(): pl.pallas_call(kernel, out_shape=(jax.ShapeDtypeStruct((256, 8, 128), F32...  92.5 us
    another operation x3, other arithmetic, shards(): r_factor = lax.linalg.cholesky(gram, symmetrize_input=False).T  12.4 us
    unnamed x12, local copies, waits for them, and re-layouts  5.74 us

profile of v1, /device:TPU:0, one launch (start us, length us, event | category | flops | bytes accessed | tf_op | source)
XLA Modules:
  0.0 112.0 jit_solution(11589144910638918323)
XLA Ops:
  0.6 0.0 copy-start.4
  0.6 0.6 copy-done.4
  1.3 0.0 copy-start
  1.3 1.2 %copy-done = f32[64,4,8,128]{3,2,1,0:T(8,128)S(1)} copy-done((f32[64,4,8,128]{3,2,1,0:T(8,128)S(1)}, f32[64,4,8,128]{3,2,1,0:T(8,128)}, u32[]{:S(2)}) %copy-start) | copy-done | bytes 1048600
  2.5 0.0 copy-start.1
  2.5 0.8 copy-done.1
  3.3 0.0 copy-start.2
  3.3 0.7 copy-done.2
  4.0 0.0 copy-start.3
  4.0 0.7 copy-done.3
  4.7 92.5 %range_finder.1 = (f32[256,8,128]{2,1,0:T(8,128)S(1)}, f32[128,128]{1,0:T(8,128)S(1)}) custom-call(f32[256,8,128]{2,1,0:T(8,128)S(1)} %bitcast.4, f32[3,4,8,128]{3,2,1,0:T(8,128)S(1)} %copy-done.1, s32[8,128]{1,0:T(8,128)S(1)} %copy-done.2, f32[8,128]{1,0:T(8,128)S(1)} %copy-done.3, s32[1,4]{1,0:T(1,128)S(1)} %copy-done.4), custom_call_target="tpu_custom_call" | custom-call | tf_op jit(solution)/shard_map/range_finder/pallas_call | solution.py:320
  97.2 11.7 %cholesky.18 = f32[128,128]{1,0:T(8,128)S(1)} custom-call(f32[128,128]{1,0:T(8,128)S(1)} %get-tuple-element.5), custom_call_target="Cholesky" | custom-call | tf_op jit(solution)/shard_map/cholesky | solution.py:331
  109.0 0.6 compare_reduce_fusion
  109.6 0.7 select_bitcast_fusion
  110.3 0.7 copy.7
  111.0 1.0 copy.9
  (1 shorter events, 0.0 us)
Async XLA Ops:
  0.6 0.7 copy-start.4
  1.3 1.2 %copy-start = (f32[64,4,8,128]{3,2,1,0:T(8,128)S(1)}, f32[64,4,8,128]{3,2,1,0:T(8,128)}, u32[]{:S(2)}) copy-start(f32[64,4,8,128]{3,2,1,0:T(8,128)} %param.5) | copy-start | bytes 3145732
  2.5 0.8 copy-start.1
  3.3 0.7 copy-start.2
  4.0 0.7 copy-start.3

commit v2 on v1

--- a/solution.py
+++ b/solution.py
@@ -11,6 +11,10 @@
 LEV = 4
 NG = 8
 NCOEF = 7
+UNROLLS = (7, 6, 5)
+EARLY = 2
+KW = LEV * NCOEF
+PAD = 40
 CELLS = 4 * 512 * 128
 HIGH = lax.Precision.HIGHEST
 
@@ -29,7 +33,7 @@
     om_v, halo, cond_v, wet_v, vol_v, runs_s,
     xm, xl, xr, cf, cbm, cbe,
     up_own, u_l, u_r, u_lr, u_h,
-    buf_a, buf_b, fin, part, out_v,
+    buf, fin, part, out_v,
     red_c, red_x, red_y, red_z,
     lsem, osem, hs, hr, ss, sr, es, er, us, ur, fs, fr, vs, vr, cs, cr, xs, xrs, ys, yr, zs, zr,
 ):
@@ -56,7 +60,7 @@
         pltpu.make_async_copy(wet, wet_v, lsem.at[1]),
         pltpu.make_async_copy(runs, runs_s, lsem.at[2]),
         pltpu.make_async_copy(vol, vol_v, lsem.at[3]),
-        pltpu.make_async_copy(om, om_v, lsem.at[4]),
+        pltpu.make_async_copy(om, om_v.at[:, pl.ds(0, LEV)], lsem.at[4]),
     ]
     for cp in loads:
         cp.start()
@@ -97,28 +101,31 @@
         cp.start()
 
     def halo_copy(g, d):
-        blk = pl.ds(g * 32, 32)
+        blk = pl.ds(g * 8, 8)
         half = pl.ds(4 * d, 4)
         return remote(
-            om.at[blk, half, :], halo.at[blk, half, :], hs.at[g, d], hr.at[g, d], (down if d else up, v)
+            om.at[blk, :, half, :], halo.at[blk, pl.ds(0, LEV), half, :], hs.at[g, d], hr.at[g, d], (down if d else up, v)
         )
 
-    for g in range(NG):
+    def send_halos(g, c):
         for d in range(2):
             halo_copy(g, d).start()
+        return c
+
+    lax.fori_loop(0, EARLY, send_halos, 0)
 
     for cp in loads[3:]:
         cp.wait()
-    om2 = om_v.reshape(2048, 128)
-    halo2 = halo.reshape(2048, 128)
-    out2 = out_v.reshape(2048, 128)
+    om2 = om_v.reshape(64 * PAD, 128)
+    halo2 = halo.reshape(64 * PAD, 128)
+    out2 = out_v.reshape(64 * PAD, 128)
 
     def pack(g, c):
         for h in range(2):
             acc = jnp.zeros((8, 128), F32)
             for k in range(16):
                 row = (k // 4) * 8 + 4 * h + k % 4
-                val = om2[pl.ds(g * 256 + row, 8, stride=32), :]
+                val = om2[pl.ds(g * 8 * PAD + row, 8, stride=PAD), :]
                 acc = jnp.where(cols // 8 == k, pltpu.roll(val, (k * 8 + 4) % 128, 1), acc)
             up_own[h, g] = acc
         return c
@@ -155,6 +162,7 @@
     ]
     for cp in fwd:
         cp.start()
+    lax.fori_loop(EARLY, NG, send_halos, 0)
 
     for cp in stat_e:
         cp.wait_recv()
@@ -196,30 +204,27 @@
         return remote(fin.at[pl.ds(w * 16, 16), grp, :], part.at[:, grp, :], vs.at[g], vr.at[g], (t, w))
 
     def out_copy(g):
-        blk = pl.ds(g * 32, 32)
-        return pltpu.make_async_copy(out_v.at[blk], out.at[blk], osem.at[g])
+        blk = pl.ds(g * 8, 8)
+        return pltpu.make_async_copy(out_v.at[blk, pl.ds(0, LEV)], out.at[blk], osem.at[g])
 
     def group(g, c):
         for d in range(2):
             halo_copy(g, d).wait_recv()
-        for r in range(16):
-            own_row = 4 <= r < 12
-            hr_ = (r - 4) if own_row else (r + 4 if r < 4 else r - 12)
-            src = om2 if own_row else halo2
-            upk = u_lr if own_row else u_h
-            wm = cbm[r, LEV * NCOEF]
-            we = cbe[r, LEV * NCOEF]
-            pk = upk[hr_ // 4, g]
-            for l in range(LEV):
-                k = l * 4 + hr_ % 4
-                buf_a[r, 2 * l] = wm * src[pl.ds(g * 256 + l * 8 + hr_, 8, stride=32), :]
-                buf_a[r, 2 * l + 1] = we * pltpu.roll(pk, (256 - (k * 8 + 4)) % 128, 1)
-        bufs = (buf_a, buf_b)
-        for p in range(4):
-            src, dst = bufs[p % 2], bufs[(p + 1) % 2]
-
-            def one_row(r, c, src=src, dst=dst, final=(p == 3)):
-                mid = [[src[r, 2 * l + e] for e in range(2)] for l in range(LEV)]
+        def load_row(i, c):
+            at = g * 8 * PAD + i
+            for src, upk, r in ((om2, u_lr, i + 4), (halo2, u_h, lax.rem(i + 12, 16))):
+                pk = upk[i // 4, g]
+                for l in range(LEV):
+                    k = l * 4 + lax.rem(i, 4)
+                    buf[0, r, 2 * l] = cbm[r, KW] * src[pl.ds(at + l * 8, 8, stride=PAD), :]
+                    buf[0, r, 2 * l + 1] = cbe[r, KW] * pltpu.roll(pk, lax.rem(252 - k * 8, 128), 1)
+            return c
+
+        lax.fori_loop(0, 8, load_row, 0)
+
+        def rows_at(src, dst, rs, final):
+            for r in rs:
+                mid = [[buf[src, r, 2 * l + e] for e in range(2)] for l in range(LEV)]
                 for l in range(LEV):
                     for e in range(1 if final else 2):
                         cb = cbe if e else cbm
@@ -228,22 +233,32 @@
                         f_r = pltpu.roll(jnp.where(first, other, me), 127, 1)
                         k = l * NCOEF
                         acc = cb[r, k] * me
-                        acc += cb[r, k + 1] * src[r - 1, 2 * l + e]
-                        acc += cb[r, k + 2] * src[r + 1, 2 * l + e]
-                        acc += cb[r, k + 3] * f_l
-                        acc += cb[r, k + 4] * f_r
+                        acc += cb[r, k + 1] * buf[src, r - 1, 2 * l + e] + cb[r, k + 2] * buf[src, r + 1, 2 * l + e]
                         if l > 0:
                             acc += cb[r, k + 5] * mid[l - 1][e]
                         if l < 3:
                             acc += cb[r, k + 6] * mid[l + 1][e]
+                        acc += cb[r, k + 3] * f_l + cb[r, k + 4] * f_r
                         if final:
                             fin[l * 8 + r - 4, pl.ds(pl.multiple_of(g * 8, 8), 8), :] = acc
-                            out2[pl.ds(g * 256 + l * 8 + r - 4, 8, stride=32), :] = acc
+                            out2[pl.ds(g * 8 * PAD + l * 8 + r - 4, 8, stride=PAD), :] = acc
                         else:
-                            dst[r, 2 * l + e] = acc
+                            buf[dst, r, 2 * l + e] = acc
+
+        for p in range(3):
+            size = UNROLLS[p]
+
+            def step(i, c, p=p, size=size):
+                rows_at(p % 2, 1 - p % 2, [1 + p + size * i + j for j in range(size)], False)
                 return c
 
-            lax.fori_loop(1 + p, 15 - p, one_row, 0)
+            lax.fori_loop(0, (14 - 2 * p) // size, step, 0)
+
+        def last_pass(i, c):
+            rows_at(1, 0, [4 + 4 * i + j for j in range(4)], True)
+            return c
+
+        lax.fori_loop(0, 2, last_pass, 0)
         vec_copy(g).start()
         out_copy(g).start()
         return c
@@ -306,12 +321,12 @@
     vm = lambda *s: pltpu.VMEM(s, F32)
     dma = lambda *s: pltpu.SemaphoreType.DMA(s)
     scratch = [
-        vm(256, 8, 128), vm(256, 8, 128), vm(3, 4, 8, 128), pltpu.VMEM((8, 128), jnp.int32), vm(8, 128),
+        vm(64, 5, 8, 128), vm(64, 5, 8, 128), vm(3, 4, 8, 128), pltpu.VMEM((8, 128), jnp.int32), vm(8, 128),
         pltpu.SMEM((1, 4), jnp.int32),
         vm(13, 16, 128), vm(13, 16, 128), vm(13, 16, 128), vm(2, 29, 16, 128),
         vm(16, 29, 8, 128), vm(16, 29, 8, 128),
         vm(2, 8, 8, 128), vm(2, 8, 8, 128), vm(2, 8, 8, 128), vm(2, 8, 8, 128), vm(2, 8, 8, 128),
-        vm(16, 8, 8, 128), vm(16, 8, 8, 128), vm(32, 64, 128), vm(16, 64, 128), vm(256, 8, 128),
+        vm(2, 16, 8, 8, 128), vm(32, 64, 128), vm(16, 64, 128), vm(64, 5, 8, 128),
         vm(2, 64, 128), vm(4, 64, 128), vm(4, 64, 128), vm(4, 64, 128),
         dma(5), dma(8), dma(8, 2), dma(8, 2), dma(4), dma(4), dma(2), dma(2), dma(2), dma(2),
         dma(2), dma(2), dma(8), dma(8), dma(1), dma(1), dma(3), dma(3), dma(3), dma(3), dma(3), dma(3),
@@ -319,7 +334,7 @@
     anys = pl.BlockSpec(memory_space=pl.ANY)
     diffused, gram = pl.pallas_call(
         kernel,
-        out_shape=(jax.ShapeDtypeStruct((256, 8, 128), F32), jax.ShapeDtypeStruct((128, 128), F32)),
+        out_shape=(jax.ShapeDtypeStruct((64, LEV, 8, 128), F32), jax.ShapeDtypeStruct((128, 128), F32)),
         in_specs=[anys] * 5,
         out_specs=(anys, pl.BlockSpec(memory_space=pltpu.VMEM)),
         scratch_shapes=scratch,
@@ -327,9 +342,9 @@
             collective_id=0, has_side_effects=True, vmem_limit_bytes=48 * 1024 * 1024
         ),
         name="range_finder",
-    )(omega.reshape(256, 8, 128), conductance, wet, volume, face_runs)
+    )(omega, conductance, wet, volume, face_runs)
     r_factor = lax.linalg.cholesky(gram, symmetrize_input=False).T
-    return (diffused.reshape(omega.shape), r_factor)
+    return (diffused, r_factor)
 
 
 def solution(mesh):

time: 112 us -> 84.8 us (0.76)
  Pallas kernels: 92.5 us -> 65.1 us
    pallas_call x1, Pallas kernels: 92.5 us -> 65.1 us  [shards(): pl.pallas_call(kernel, out_shape=(jax.ShapeDtypeStruct((64, LEV, 8, 128),...]
where the time goes in v2:
time: 84.8 us; the launch traced here: 84.5 us
  Pallas kernels  65.1 us (77%)
  other arithmetic  13 us (15%)
  local copies, waits for them, and re-layouts  5.74 us (7%)
    pallas_call x1, Pallas kernels, shards(): pl.pallas_call(kernel, out_shape=(jax.ShapeDtypeStruct((64, LEV, 8, 128),...  65.1 us
    another operation x3, other arithmetic, shards(): r_factor = lax.linalg.cholesky(gram, symmetrize_input=False).T  12.4 us
    unnamed x12, local copies, waits for them, and re-layouts  5.74 us

profile of v2, /device:TPU:0, one launch (start us, length us, event | category | flops | bytes accessed | tf_op | source)
XLA Modules:
  0.0 84.5 jit_solution(1182356217594318663)
XLA Ops:
  0.6 0.0 copy-start
  0.6 1.2 %copy-done = f32[64,4,8,128]{3,2,1,0:T(8,128)S(1)} copy-done((f32[64,4,8,128]{3,2,1,0:T(8,128)S(1)}, f32[64,4,8,128]{3,2,1,0:T(8,128)}, u32[]{:S(2)}) %copy-start) | copy-done | bytes 1048600
  1.9 0.0 copy-start.1
  1.9 0.8 copy-done.1
  2.7 0.0 copy-start.2
  2.7 0.7 copy-done.2
  3.3 0.0 copy-start.3
  3.3 0.7 copy-done.3
  4.0 0.0 copy-start.4
  4.0 0.7 copy-done.4
  4.7 65.1 %range_finder.1 = (f32[64,4,8,128]{3,2,1,0:T(8,128)S(1)}, f32[128,128]{1,0:T(8,128)S(1)}) custom-call(f32[64,4,8,128]{3,2,1,0:T(8,128)S(1)} %copy-done, f32[3,4,8,128]{3,2,1,0:T(8,128)S(1)} %copy-done.1, s32[8,128]{1,0:T(8,128)S(1)} %copy-done.2, f32[8,128]{1,0:T(8,128)S(1)} %copy-done.3, s32[1,4]{1,0:T(1,128)S(1)} %copy-done.4), custom_call_target="tpu_custom_call" | custom-call | tf_op jit(solution)/shard_map/range_finder/pallas_call | solution.py:335
  69.7 11.7 %cholesky.18 = f32[128,128]{1,0:T(8,128)S(1)} custom-call(f32[128,128]{1,0:T(8,128)S(1)} %get-tuple-element.5), custom_call_target="Cholesky" | custom-call | tf_op jit(solution)/shard_map/cholesky | solution.py:346
  81.5 0.6 compare_reduce_fusion
  82.1 0.7 select_bitcast_fusion
  82.8 0.7 copy.7
  83.5 1.0 %copy.9 = f32[64,4,8,128]{3,2,1,0:T(8,128)} copy(f32[64,4,8,128]{3,2,1,0:T(8,128)S(1)} %get-tuple-element.10) | data formatting | bytes 2097152
  (1 shorter events, 0.0 us)
Async XLA Ops:
  0.6 1.2 %copy-start = (f32[64,4,8,128]{3,2,1,0:T(8,128)S(1)}, f32[64,4,8,128]{3,2,1,0:T(8,128)}, u32[]{:S(2)}) copy-start(f32[64,4,8,128]{3,2,1,0:T(8,128)} %om.1) | copy-start | bytes 3145732
  1.9 0.8 copy-start.1
  2.7 0.7 copy-start.2
  3.3 0.7 copy-start.3
  4.0 0.7 copy-start.4

commit v3 on v2

--- a/solution.py
+++ b/solution.py
@@ -12,8 +12,9 @@
 NG = 8
 NCOEF = 7
 UNROLLS = (7, 6, 5)
-EARLY = 2
+EARLY = 4
 KW = LEV * NCOEF
+GRAM_ROWS = 4
 PAD = 40
 CELLS = 4 * 512 * 128
 HIGH = lax.Precision.HIGHEST
@@ -33,9 +34,9 @@
     om_v, halo, cond_v, wet_v, vol_v, runs_s,
     xm, xl, xr, cf, cbm, cbe,
     up_own, u_l, u_r, u_lr, u_h,
-    buf, fin, part, out_v,
+    buf, fin, part,
     red_c, red_x, red_y, red_z,
-    lsem, osem, hs, hr, ss, sr, es, er, us, ur, fs, fr, vs, vr, cs, cr, xs, xrs, ys, yr, zs, zr,
+    lsem, hs, hr, ss, sr, es, er, us, ur, fs, fr, vs, vr, cs, cr, xs, xrs, ys, yr, zs, zr,
 ):
     t = lax.axis_index("tiles")
     v = lax.axis_index("vec")
@@ -118,7 +119,7 @@
         cp.wait()
     om2 = om_v.reshape(64 * PAD, 128)
     halo2 = halo.reshape(64 * PAD, 128)
-    out2 = out_v.reshape(64 * PAD, 128)
+    out2 = out.reshape(64 * 32, 128)
 
     def pack(g, c):
         for h in range(2):
@@ -202,10 +203,6 @@
     def vec_copy(g):
         grp = pl.ds(pl.multiple_of(g * 8, 8), 8)
         return remote(fin.at[pl.ds(w * 16, 16), grp, :], part.at[:, grp, :], vs.at[g], vr.at[g], (t, w))
-
-    def out_copy(g):
-        blk = pl.ds(g * 8, 8)
-        return pltpu.make_async_copy(out_v.at[blk, pl.ds(0, LEV)], out.at[blk], osem.at[g])
 
     def group(g, c):
         for d in range(2):
@@ -241,7 +238,7 @@
                         acc += cb[r, k + 3] * f_l + cb[r, k + 4] * f_r
                         if final:
                             fin[l * 8 + r - 4, pl.ds(pl.multiple_of(g * 8, 8), 8), :] = acc
-                            out2[pl.ds(g * 8 * PAD + l * 8 + r - 4, 8, stride=PAD), :] = acc
+                            out2[pl.ds(g * 256 + l * 8 + r - 4, 8, stride=32), :] = acc
                         else:
                             buf[dst, r, 2 * l + e] = acc
 
@@ -260,26 +257,31 @@
 
         lax.fori_loop(0, 2, last_pass, 0)
         vec_copy(g).start()
-        out_copy(g).start()
         return c
 
     lax.fori_loop(0, NG, group, 0)
 
+    def wide(take, i):
+        return jnp.concatenate([take(i * GRAM_ROWS + j) for j in range(GRAM_ROWS)], axis=1)
+
+    def weights(i):
+        return wide(lambda k: vol_v[pl.ds(lax.rem(k, 8), 1), :], i)
+
     def own_block(i, acc):
-        a = fin[i]
-        return acc + nt_dot(a * vol_v[pl.ds(lax.rem(i, 8), 1), :], a)
-
-    g_own = lax.fori_loop(0, 32, own_block, jnp.zeros((64, 64), F32))
+        a = wide(lambda k: fin[k], i)
+        return acc + nt_dot(a * weights(i), a)
+
+    g_own = lax.fori_loop(0, 32 // GRAM_ROWS, own_block, jnp.zeros((64, 64), F32))
     for g in range(NG):
         vec_copy(g).wait_recv()
 
     def cross_block(i, acc):
-        mine, theirs = fin[v * 16 + i], part[i]
+        mine, theirs = wide(lambda k: fin[v * 16 + k], i), wide(lambda k: part[k], i)
         a = jnp.where(v == 0, mine, theirs)
         b = jnp.where(v == 0, theirs, mine)
-        return acc + nt_dot(a * vol_v[pl.ds(lax.rem(i, 8), 1), :], b)
-
-    g_cross = lax.fori_loop(0, 16, cross_block, jnp.zeros((64, 64), F32))
+        return acc + nt_dot(a * weights(i), b)
+
+    g_cross = lax.fori_loop(0, 16 // GRAM_ROWS, cross_block, jnp.zeros((64, 64), F32))
 
     def stage(val, red, slot, peers, s, r):
         red[slot] = val
@@ -314,7 +316,6 @@
         for d in range(2):
             halo_copy(g, d).wait_send()
         vec_copy(g).wait_send()
-        out_copy(g).wait()
 
 
 def shards(omega, conductance, wet, volume, face_runs):
@@ -326,9 +327,9 @@
         vm(13, 16, 128), vm(13, 16, 128), vm(13, 16, 128), vm(2, 29, 16, 128),
         vm(16, 29, 8, 128), vm(16, 29, 8, 128),
         vm(2, 8, 8, 128), vm(2, 8, 8, 128), vm(2, 8, 8, 128), vm(2, 8, 8, 128), vm(2, 8, 8, 128),
-        vm(2, 16, 8, 8, 128), vm(32, 64, 128), vm(16, 64, 128), vm(64, 5, 8, 128),
+        vm(2, 16, 8, 8, 128), vm(32, 64, 128), vm(16, 64, 128),
         vm(2, 64, 128), vm(4, 64, 128), vm(4, 64, 128), vm(4, 64, 128),
-        dma(5), dma(8), dma(8, 2), dma(8, 2), dma(4), dma(4), dma(2), dma(2), dma(2), dma(2),
+        dma(5), dma(8, 2), dma(8, 2), dma(4), dma(4), dma(2), dma(2), dma(2), dma(2),
         dma(2), dma(2), dma(8), dma(8), dma(1), dma(1), dma(3), dma(3), dma(3), dma(3), dma(3), dma(3),
     ]
     anys = pl.BlockSpec(memory_space=pl.ANY)
@@ -336,10 +337,10 @@
         kernel,
         out_shape=(jax.ShapeDtypeStruct((64, LEV, 8, 128), F32), jax.ShapeDtypeStruct((128, 128), F32)),
         in_specs=[anys] * 5,
-        out_specs=(anys, pl.BlockSpec(memory_space=pltpu.VMEM)),
+        out_specs=(pl.BlockSpec(memory_space=pltpu.VMEM),) * 2,
         scratch_shapes=scratch,
         compiler_params=pltpu.CompilerParams(
-            collective_id=0, has_side_effects=True, vmem_limit_bytes=48 * 1024 * 1024
+            collective_id=0, has_side_effects=True, vmem_limit_bytes=67043328
         ),
         name="range_finder",
     )(omega, conductance, wet, volume, face_runs)

time: 84.8 us -> 82.4 us (0.972)
  local copies, waits for them, and re-layouts: 5.74 us -> 2.99 us
  other arithmetic: 13 us -> 13.9 us
    unnamed x12 -> x2, local copies, waits for them, and re-layouts: 5.74 us -> 2.99 us
where the time goes in v3:
time: 82.4 us; the launch traced here: 82.1 us
  Pallas kernels  64.6 us (78%)
  other arithmetic  13.9 us (17%)
  local copies, waits for them, and re-layouts  2.99 us (4%)
    pallas_call x1, Pallas kernels, shards(): pl.pallas_call(kernel, out_shape=(jax.ShapeDtypeStruct((64, LEV, 8, 128),...  64.6 us
    another operation x3, other arithmetic, shards(): r_factor = lax.linalg.cholesky(gram, symmetrize_input=False).T  13.2 us
    unnamed x2, local copies, waits for them, and re-layouts  2.99 us

profile of v3, /device:TPU:0, one launch (start us, length us, event | category | flops | bytes accessed | tf_op | source)
XLA Modules:
  0.0 82.1 jit_solution(14377590589115424713)
XLA Ops:
  0.6 64.6 %range_finder.1 = (f32[64,4,8,128]{3,2,1,0:T(8,128)}, f32[128,128]{1,0:T(8,128)}) custom-call(f32[64,4,8,128]{3,2,1,0:T(8,128)} %om.1, f32[3,4,8,128]{3,2,1,0:T(8,128)} %cond.1, s32[8,128]{1,0:T(8,128)} %wet.1, f32[8,128]{1,0:T(8,128)} %vol.1, s32[1,4]{1,0:T(1,128)} %runs.1), custom_call_target="tpu_custom_call" | custom-call | tf_op jit(solution)/shard_map/range_finder/pallas_call | solution.py:336
  65.3 12.5 %cholesky.18 = f32[128,128]{1,0:T(8,128)S(1)} custom-call(f32[128,128]{1,0:T(8,128)} %get-tuple-element.5), custom_call_target="Cholesky" | custom-call | tf_op jit(solution)/shard_map/cholesky | solution.py:347
  77.9 0.6 compare_reduce_fusion
  78.5 0.7 select_bitcast_fusion
  79.2 0.7 copy.7
  79.9 2.3 %copy.9 = f32[64,4,8,128]{3,2,1,0:T(8,128)} copy(f32[64,4,8,128]{3,2,1,0:T(8,128)} %get-tuple-element.10) | data formatting | bytes 2097152
  (1 shorter events, 0.0 us)

commit v4 on v3

--- a/solution.py
+++ b/solution.py
@@ -15,6 +15,7 @@
 EARLY = 4
 KW = LEV * NCOEF
 GRAM_ROWS = 4
+PANEL = 16
 PAD = 40
 CELLS = 4 * 512 * 128
 HIGH = lax.Precision.HIGHEST
@@ -318,6 +319,61 @@
         vec_copy(g).wait_send()
 
 
+def factor_kernel(gram, raw, r_out, out, a_ref, hold, sem_in, sem_out):
+    fetch = pltpu.make_async_copy(raw, hold, sem_in)
+    fetch.start()
+    a_ref[...] = gram[...]
+    row_id = lax.broadcasted_iota(jnp.int32, (PANEL, 128), 0)
+    col_id = lax.broadcasted_iota(jnp.int32, (PANEL, 128), 1)
+
+    def panel(k, c):
+        start = pl.multiple_of(k * PANEL, PANEL)
+        p = a_ref[pl.ds(start, PANEL), :]
+        front = pltpu.roll(p, lax.rem(128 - start, 128), 1)
+        cols = [jnp.broadcast_to(front[:, j : j + 1], (PANEL, 128)) for j in range(PANEL)]
+        for j in range(PANEL):
+            d = cols[j][j : j + 1, :]
+            inv = lax.rsqrt(d)
+            inv = inv * (1.5 - 0.5 * d * inv * inv)
+            below = jnp.where(row_id > j, cols[j] * inv, 0.0)
+            u = p[j : j + 1, :] * inv
+            p = jnp.where(row_id == j, u, p - below * u)
+            for m in range(j + 1, PANEL):
+                cols[m] = cols[m] - below * (cols[m][j : j + 1, :] * inv)
+        p = jnp.where(col_id >= row_id + start, p, 0.0)
+        r_out[pl.ds(start, PANEL), :] = p
+
+        @pl.when(k < 128 // PANEL - 1)
+        def _():
+            a_ref[...] -= lax.dot_general(
+                p, p, (((0,), (0,)), ((), ())), precision=HIGH, preferred_element_type=F32
+            )
+
+        return c
+
+    lax.fori_loop(0, 2, panel, 0)
+    fetch.wait()
+    put = pltpu.make_async_copy(hold, out, sem_out)
+    put.start()
+    lax.fori_loop(2, 128 // PANEL, panel, 0)
+    put.wait()
+
+
+def factor(gram, raw):
+    anys = pl.BlockSpec(memory_space=pl.ANY)
+    vmem = pl.BlockSpec(memory_space=pltpu.VMEM)
+    return pl.pallas_call(
+        factor_kernel,
+        out_shape=(jax.ShapeDtypeStruct((128, 128), F32), jax.ShapeDtypeStruct(raw.shape, F32)),
+        in_specs=[vmem, anys],
+        out_specs=(vmem, anys),
+        scratch_shapes=[
+            pltpu.VMEM((128, 128), F32), pltpu.VMEM(raw.shape, F32), pltpu.SemaphoreType.DMA, pltpu.SemaphoreType.DMA
+        ],
+        name="upper_factor",
+    )(gram, raw)
+
+
 def shards(omega, conductance, wet, volume, face_runs):
     vm = lambda *s: pltpu.VMEM(s, F32)
     dma = lambda *s: pltpu.SemaphoreType.DMA(s)
@@ -344,7 +400,7 @@
         ),
         name="range_finder",
     )(omega, conductance, wet, volume, face_runs)
-    r_factor = lax.linalg.cholesky(gram, symmetrize_input=False).T
+    r_factor, diffused = factor(gram, diffused)
     return (diffused, r_factor)
 
 

time: 82.4 us -> 71.8 us (0.87)
  other arithmetic: 13.9 us -> 0 us
  Pallas kernels: 64.6 us -> 71 us
  local copies, waits for them, and re-layouts: 2.99 us -> 0 us
    another operation x3 -> x0, other arithmetic: 13.2 us -> none  [shards(): r_factor = lax.linalg.cholesky(gram, symmetrize_input=False).T]
    pallas_call x0 -> x1, Pallas kernels: none -> 6.36 us  [factor(): pl.pallas_call(factor_kernel, out_shape=(jax.ShapeDtypeStruct((128, 128),...]
    unnamed x2 -> x0, local copies, waits for them, and re-layouts: 2.99 us -> none
where the time goes in v4:
time: 71.8 us; the launch traced here: 71.6 us
  Pallas kernels  71 us (99%)
    pallas_call x1, Pallas kernels, shards(): pl.pallas_call(kernel, out_shape=(jax.ShapeDtypeStruct((64, LEV, 8, 128),...  64.6 us
    pallas_call x1, Pallas kernels, factor(): pl.pallas_call(factor_kernel, out_shape=(jax.ShapeDtypeStruct((128, 128),...  6.36 us

profile of v4, /device:TPU:0, one launch (start us, length us, event | category | flops | bytes accessed | tf_op | source)
XLA Modules:
  0.0 71.6 jit_solution(14448384837581541947)
XLA Ops:
  0.6 64.6 %range_finder.1 = (f32[64,4,8,128]{3,2,1,0:T(8,128)}, f32[128,128]{1,0:T(8,128)}) custom-call(f32[64,4,8,128]{3,2,1,0:T(8,128)} %om.1, f32[3,4,8,128]{3,2,1,0:T(8,128)} %cond.1, s32[8,128]{1,0:T(8,128)} %wet.1, f32[8,128]{1,0:T(8,128)} %vol.1, s32[1,4]{1,0:T(1,128)} %runs.1), custom_call_target="tpu_custom_call" | custom-call | tf_op jit(solution)/shard_map/range_finder/pallas_call | solution.py:392
  65.3 6.4 %upper_factor.1 = (f32[128,128]{1,0:T(8,128)}, f32[64,4,8,128]{3,2,1,0:T(8,128)}) custom-call(f32[128,128]{1,0:T(8,128)} %get-tuple-element.6.gram, f32[64,4,8,128]{3,2,1,0:T(8,128)} %get-tuple-element.7.raw), custom_call_target="tpu_custom_call" | custom-call | tf_op jit(solution)/shard_map/upper_factor/pallas_call | solution.py:365

commit v5 on v4

--- a/solution.py
+++ b/solution.py
@@ -14,7 +14,7 @@
 UNROLLS = (7, 6, 5)
 EARLY = 4
 KW = LEV * NCOEF
-GRAM_ROWS = 4
+GRAM_ROWS = 8
 PANEL = 16
 PAD = 40
 CELLS = 4 * 512 * 128
@@ -35,9 +35,9 @@
     om_v, halo, cond_v, wet_v, vol_v, runs_s,
     xm, xl, xr, cf, cbm, cbe,
     up_own, u_l, u_r, u_lr, u_h,
-    buf, fin, part,
+    buf, fin, part, out_v,
     red_c, red_x, red_y, red_z,
-    lsem, hs, hr, ss, sr, es, er, us, ur, fs, fr, vs, vr, cs, cr, xs, xrs, ys, yr, zs, zr,
+    lsem, osem, hs, hr, ss, sr, es, er, us, ur, fs, fr, vs, vr, cs, cr, xs, xrs, ys, yr, zs, zr,
 ):
     t = lax.axis_index("tiles")
     v = lax.axis_index("vec")
@@ -120,7 +120,7 @@
         cp.wait()
     om2 = om_v.reshape(64 * PAD, 128)
     halo2 = halo.reshape(64 * PAD, 128)
-    out2 = out.reshape(64 * 32, 128)
+    out2 = out_v.reshape(64 * PAD, 128)
 
     def pack(g, c):
         for h in range(2):
@@ -204,6 +204,10 @@
     def vec_copy(g):
         grp = pl.ds(pl.multiple_of(g * 8, 8), 8)
         return remote(fin.at[pl.ds(w * 16, 16), grp, :], part.at[:, grp, :], vs.at[g], vr.at[g], (t, w))
+
+    def out_copy(g):
+        blk = pl.ds(g * 8, 8)
+        return pltpu.make_async_copy(out_v.at[blk, pl.ds(0, LEV)], out.at[blk], osem.at[g])
 
     def group(g, c):
         for d in range(2):
@@ -239,7 +243,7 @@
                         acc += cb[r, k + 3] * f_l + cb[r, k + 4] * f_r
                         if final:
                             fin[l * 8 + r - 4, pl.ds(pl.multiple_of(g * 8, 8), 8), :] = acc
-                            out2[pl.ds(g * 256 + l * 8 + r - 4, 8, stride=32), :] = acc
+                            out2[pl.ds(g * 8 * PAD + l * 8 + r - 4, 8, stride=PAD), :] = acc
                         else:
                             buf[dst, r, 2 * l + e] = acc
 
@@ -258,6 +262,7 @@
 
         lax.fori_loop(0, 2, last_pass, 0)
         vec_copy(g).start()
+        out_copy(g).start()
         return c
 
     lax.fori_loop(0, NG, group, 0)
@@ -317,6 +322,7 @@
         for d in range(2):
             halo_copy(g, d).wait_send()
         vec_copy(g).wait_send()
+        out_copy(g).wait()
 
 
 def factor_kernel(gram, raw, r_out, out, a_ref, hold, sem_in, sem_out):
@@ -383,9 +389,9 @@
         vm(13, 16, 128), vm(13, 16, 128), vm(13, 16, 128), vm(2, 29, 16, 128),
         vm(16, 29, 8, 128), vm(16, 29, 8, 128),
         vm(2, 8, 8, 128), vm(2, 8, 8, 128), vm(2, 8, 8, 128), vm(2, 8, 8, 128), vm(2, 8, 8, 128),
-        vm(2, 16, 8, 8, 128), vm(32, 64, 128), vm(16, 64, 128),
+        vm(2, 16, 8, 8, 128), vm(32, 64, 128), vm(16, 64, 128), vm(64, 5, 8, 128),
         vm(2, 64, 128), vm(4, 64, 128), vm(4, 64, 128), vm(4, 64, 128),
-        dma(5), dma(8, 2), dma(8, 2), dma(4), dma(4), dma(2), dma(2), dma(2), dma(2),
+        dma(5), dma(8), dma(8, 2), dma(8, 2), dma(4), dma(4), dma(2), dma(2), dma(2), dma(2),
         dma(2), dma(2), dma(8), dma(8), dma(1), dma(1), dma(3), dma(3), dma(3), dma(3), dma(3), dma(3),
     ]
     anys = pl.BlockSpec(memory_space=pl.ANY)
@@ -393,7 +399,7 @@
         kernel,
         out_shape=(jax.ShapeDtypeStruct((64, LEV, 8, 128), F32), jax.ShapeDtypeStruct((128, 128), F32)),
         in_specs=[anys] * 5,
-        out_specs=(pl.BlockSpec(memory_space=pltpu.VMEM),) * 2,
+        out_specs=(anys, pl.BlockSpec(memory_space=pltpu.VMEM)),
         scratch_shapes=scratch,
         compiler_params=pltpu.CompilerParams(
             collective_id=0, has_side_effects=True, vmem_limit_bytes=67043328

time: 71.8 us -> 71 us (0.989)
  Pallas kernels: 71 us -> 70.2 us
    pallas_call x1, Pallas kernels: 64.6 us -> 63.8 us  [shards(): pl.pallas_call(kernel, out_shape=(jax.ShapeDtypeStruct((64, LEV, 8, 128),...]
where the time goes in v5:
time: 71 us; the launch traced here: 70.8 us
  Pallas kernels  70.2 us (99%)
    pallas_call x1, Pallas kernels, shards(): pl.pallas_call(kernel, out_shape=(jax.ShapeDtypeStruct((64, LEV, 8, 128),...  63.8 us
    pallas_call x1, Pallas kernels, factor(): pl.pallas_call(factor_kernel, out_shape=(jax.ShapeDtypeStruct((128, 128),...  6.37 us

profile of v5, /device:TPU:0, one launch (start us, length us, event | category | flops | bytes accessed | tf_op | source)
XLA Modules:
  0.0 70.8 jit_solution(3115361439171672292)
XLA Ops:
  0.6 63.8 %range_finder.1 = (f32[64,4,8,128]{3,2,1,0:T(8,128)}, f32[128,128]{1,0:T(8,128)}) custom-call(f32[64,4,8,128]{3,2,1,0:T(8,128)} %om.1, f32[3,4,8,128]{3,2,1,0:T(8,128)} %cond.1, s32[8,128]{1,0:T(8,128)} %wet.1, f32[8,128]{1,0:T(8,128)} %vol.1, s32[1,4]{1,0:T(1,128)} %runs.1), custom_call_target="tpu_custom_call" | custom-call | tf_op jit(solution)/shard_map/range_finder/pallas_call | solution.py:398
  64.4 6.4 %upper_factor.1 = (f32[128,128]{1,0:T(8,128)}, f32[64,4,8,128]{3,2,1,0:T(8,128)}) custom-call(f32[128,128]{1,0:T(8,128)} %get-tuple-element.6.gram, f32[64,4,8,128]{3,2,1,0:T(8,128)} %get-tuple-element.7.raw), custom_call_target="tpu_custom_call" | custom-call | tf_op jit(solution)/shard_map/upper_factor/pallas_call | solution.py:371

commit v6 on v5

--- a/solution.py
+++ b/solution.py
@@ -222,7 +222,7 @@
                     buf[0, r, 2 * l + 1] = cbe[r, KW] * pltpu.roll(pk, lax.rem(252 - k * 8, 128), 1)
             return c
 
-        lax.fori_loop(0, 8, load_row, 0)
+        lax.fori_loop(0, 8, load_row, 0, unroll=2)
 
         def rows_at(src, dst, rs, final):
             for r in rs:
@@ -257,10 +257,10 @@
             lax.fori_loop(0, (14 - 2 * p) // size, step, 0)
 
         def last_pass(i, c):
-            rows_at(1, 0, [4 + 4 * i + j for j in range(4)], True)
+            rows_at(1, 0, [4 + 8 * i + j for j in range(8)], True)
             return c
 
-        lax.fori_loop(0, 2, last_pass, 0)
+        lax.fori_loop(0, 1, last_pass, 0)
         vec_copy(g).start()
         out_copy(g).start()
         return c

time: 71 us -> 68.4 us (0.963)
  Pallas kernels: 70.2 us -> 67.6 us
    pallas_call x1, Pallas kernels: 63.8 us -> 61.2 us  [shards(): pl.pallas_call(kernel, out_shape=(jax.ShapeDtypeStruct((64, LEV, 8, 128),...]
where the time goes in v6:
time: 68.4 us; the launch traced here: 68.2 us
  Pallas kernels  67.6 us (99%)
    pallas_call x1, Pallas kernels, shards(): pl.pallas_call(kernel, out_shape=(jax.ShapeDtypeStruct((64, LEV, 8, 128),...  61.2 us
    pallas_call x1, Pallas kernels, factor(): pl.pallas_call(factor_kernel, out_shape=(jax.ShapeDtypeStruct((128, 128),...  6.37 us

profile of v6, /device:TPU:0, one launch (start us, length us, event | category | flops | bytes accessed | tf_op | source)
XLA Modules:
  0.0 68.2 jit_solution(17971304260427375821)
XLA Ops:
  0.6 61.2 %range_finder.1 = (f32[64,4,8,128]{3,2,1,0:T(8,128)}, f32[128,128]{1,0:T(8,128)}) custom-call(f32[64,4,8,128]{3,2,1,0:T(8,128)} %om.1, f32[3,4,8,128]{3,2,1,0:T(8,128)} %cond.1, s32[8,128]{1,0:T(8,128)} %wet.1, f32[8,128]{1,0:T(8,128)} %vol.1, s32[1,4]{1,0:T(1,128)} %runs.1), custom_call_target="tpu_custom_call" | custom-call | tf_op jit(solution)/shard_map/range_finder/pallas_call | solution.py:398
  61.9 6.4 %upper_factor.1 = (f32[128,128]{1,0:T(8,128)}, f32[64,4,8,128]{3,2,1,0:T(8,128)}) custom-call(f32[128,128]{1,0:T(8,128)} %get-tuple-element.6.gram, f32[64,4,8,128]{3,2,1,0:T(8,128)} %get-tuple-element.7.raw), custom_call_target="tpu_custom_call" | custom-call | tf_op jit(solution)/shard_map/upper_factor/pallas_call | solution.py:371
